TPU v7x, 32 devices: a whole 2x2x4 slice. The times are simulated.
32 devices in a mesh: groups: 2 (over y), blk: 8 (over z, x), uly: 2 (over core).
Axes of the slice: x: 2, y: 2, z: 4, core: 2. Of those that a mesh axis runs over, the one named last changes fastest.
Arguments:
- query_proj: bfloat16 [4096, 4096], P(('groups', 'blk', 'uly')), parts along dimension 0, may hold values from -17 to 17
- key_proj: bfloat16 [4096, 512], P(('groups', 'blk', 'uly')), parts along dimension 0, may hold values from -17 to 17
- value_projection: bfloat16 [4096, 512], P(('groups', 'blk', 'uly')), parts along dimension 0, may hold values from -6 to 6
- query_gain: float32 [128], replicated, may hold values from 0.5 to 6
- key_gain: float32 [128], replicated, may hold values from 0.5 to 6
Outputs:
- attended: bfloat16 [4096, 4096], P(('groups', 'blk', 'uly')), parts along dimension 0
There are 2 independent parts, one for each index of `groups`. A program takes and returns all parts, laid end to end along the dimension named above; an argument that names none is the same for every part. Nothing has to cross between parts.
All inputs are finite; a program needn't handle non-finite values.
Results may differ from a plain program's by a relative error of at most 0.0085.
The roundings to bfloat16 on the way count: a program that leaves them out, or rounds other values in their place, can miss the bound.
Values may be sent and summed in bfloat16 or wider, within the bound.
A program may use at most 64 MiB of HBM per device.

v0:
```python
import math

import jax
import jax.numpy as jnp
from jax import lax
from jax.sharding import PartitionSpec as P

NEG_FILL = -1e30
ROPE_BASE = 1000000.0


def shifted(block, axis, distance):
    devices = range(lax.axis_size(axis))
    route = [(i - distance, i) for i in devices if i - distance in devices]
    return lax.ppermute(block, axis, route)


def rotate_rows(source, scales, positions):
    head_width = scales.shape[0]
    row_count = source.shape[0]
    head_count = source.shape[1] // head_width
    values = source.astype(jnp.float32).reshape(row_count, head_count, head_width)
    mean_square = jnp.mean(values * values, axis=-1, keepdims=True)
    normed = values * lax.rsqrt(mean_square + 1e-06) * scales
    half_width = head_width // 2
    frequency = jnp.exp(
        jnp.arange(half_width, dtype=jnp.float32) * (-2.0 * math.log(ROPE_BASE) / head_width)
    )
    angles = positions.astype(jnp.float32)[:, None] * frequency[None, :]
    cosine = jnp.cos(angles)[:, None, :]
    sine = jnp.sin(angles)[:, None, :]
    first_half = normed[..., :half_width]
    second_half = normed[..., half_width:]
    rotated = jnp.concatenate(
        [first_half * cosine - second_half * sine, second_half * cosine + first_half * sine],
        axis=-1,
    )
    return rotated.reshape(row_count, head_count * head_width).astype(jnp.bfloat16)


def attend(running, query_rows, query_pos, key_rows, value_rows, key_pos, key_valid, window):
    top_score, total_weight, weighted = running
    row_count = query_rows.shape[0]
    key_count = key_rows.shape[0]
    head_width = weighted.shape[-1]
    kv_heads = key_rows.shape[1] // head_width
    group_count = query_rows.shape[1] // head_width // kv_heads
    query_heads = query_rows.reshape(row_count, kv_heads, group_count, head_width)
    key_heads = key_rows.reshape(key_count, kv_heads, head_width)
    value_heads = value_rows.reshape(key_count, kv_heads, head_width)
    scores = jnp.einsum(
        "rkgd,nkd->kgrn", query_heads, key_heads, preferred_element_type=jnp.float32
    ) * (1.0 / math.sqrt(head_width))
    distance = query_pos[:, None] - key_pos[None, :]
    allowed = (distance >= 0) & (distance < window) & key_valid[None, :]
    scores = jnp.where(allowed, scores, NEG_FILL)
    new_top = jnp.maximum(top_score, jnp.max(scores, axis=-1))
    weights = jnp.exp(scores - new_top[..., None])
    rescale = jnp.exp(top_score - new_top)
    total_weight = total_weight * rescale + jnp.sum(weights, axis=-1)
    weighted = weighted * rescale[..., None] + jnp.einsum(
        "kgrn,nkd->kgrd",
        weights.astype(jnp.bfloat16),
        value_heads,
        preferred_element_type=jnp.float32,
    )
    return (new_top, total_weight, weighted)


def finish(running):
    top_score, total_weight, weighted = running
    mixed_rows = weighted / total_weight[..., None]
    return (
        jnp.transpose(mixed_rows, (2, 0, 1, 3))
        .reshape(mixed_rows.shape[2], -1)
        .astype(jnp.bfloat16)
    )


def local(query_proj, key_proj, value_projection, query_gain, key_gain):
    cycle_size = lax.axis_size("blk")
    cycle_index = lax.axis_index("blk")
    stretch_len = query_proj.shape[0]
    head_width = query_gain.shape[0]
    span_steps = max(1, cycle_size // 64)
    window = span_steps * stretch_len
    last_stretch = 2 * cycle_size - 1
    offsets = jnp.arange(stretch_len, dtype=jnp.int32)
    low_pos = cycle_index * stretch_len + offsets
    high_pos = (last_stretch - cycle_index) * stretch_len + offsets
    both_pos = jnp.concatenate([low_pos, high_pos])
    query_raw, key_raw, value_all = (
        lax.all_to_all(query_proj, "uly", split_axis=1, concat_axis=0, tiled=True),
        lax.all_to_all(key_proj, "uly", split_axis=1, concat_axis=0, tiled=True),
        lax.all_to_all(value_projection, "uly", split_axis=1, concat_axis=0, tiled=True),
    )
    query_all = rotate_rows(query_raw, query_gain, both_pos)
    key_all = rotate_rows(key_raw, key_gain, both_pos)
    query_low = query_all[:stretch_len]
    query_high = query_all[stretch_len:]
    kv_heads = key_all.shape[1] // head_width
    group_count = query_all.shape[1] // head_width // kv_heads

    def fresh_state():
        return (
            jnp.full((kv_heads, group_count, stretch_len), NEG_FILL, jnp.float32),
            jnp.zeros((kv_heads, group_count, stretch_len), jnp.float32),
            jnp.zeros((kv_heads, group_count, stretch_len, head_width), jnp.float32),
        )

    low_state = attend(
        fresh_state(),
        query_low,
        low_pos,
        key_all[:stretch_len],
        value_all[:stretch_len],
        low_pos,
        jnp.ones((stretch_len,), bool),
        window,
    )
    high_state = attend(
        fresh_state(),
        query_high,
        high_pos,
        key_all,
        value_all,
        both_pos,
        jnp.ones((2 * stretch_len,), bool),
        window,
    )
    block_pair = jnp.stack([key_all, value_all])

    def send_up(payload):
        return shifted(payload, "blk", 1)

    upward = block_pair[:, :stretch_len]

    def cycle_turn(offset, carried):
        upward, downward, low_state, high_state = carried
        upward = send_up(upward)
        downward = shifted(downward, "blk", -1)
        left_index = cycle_index - offset
        right_index = cycle_index + offset
        left_pos = left_index * stretch_len + offsets
        right_low = right_index * stretch_len + offsets
        right_high = (last_stretch - right_index) * stretch_len + offsets
        left_valid = jnp.broadcast_to(left_index >= 0, (stretch_len,))
        right_valid = jnp.broadcast_to(right_index <= cycle_size - 1, (2 * stretch_len,))
        left_keys = upward[0, :stretch_len]
        left_values = upward[1, :stretch_len]
        low_state = attend(
            low_state, query_low, low_pos, left_keys, left_values, left_pos, left_valid, window
        )
        high_keys = jnp.concatenate([left_keys, downward[0]])
        high_values = jnp.concatenate([left_values, downward[1]])
        high_key_pos = jnp.concatenate([left_pos, right_low, right_high])
        high_valid = jnp.concatenate([left_valid, right_valid])
        high_state = attend(
            high_state,
            query_high,
            high_pos,
            high_keys,
            high_values,
            high_key_pos,
            high_valid,
            window,
        )
        return (upward, downward, low_state, high_state)

    carried = lax.fori_loop(
        1, span_steps + 1, cycle_turn, (upward, block_pair, low_state, high_state)
    )
    merged = jnp.concatenate([finish(carried[2]), finish(carried[3])])
    return lax.all_to_all(merged, "uly", split_axis=0, concat_axis=1, tiled=True)


def solution(mesh):
    placed = (
        P(("groups", "blk", "uly"), None),
        P(("groups", "blk", "uly"), None),
        P(("groups", "blk", "uly"), None),
        P(),
        P(),
    )
    return jax.shard_map(
        local,
        mesh=mesh,
        in_specs=placed,
        out_specs=P(("groups", "blk", "uly"), None),
        check_vma=False,
    )
```

profile of v0, /device:TPU:25, one launch (start us, length us, event | category | flops | bytes accessed | tf_op | source)
XLA Modules:
  0.0 51.0 jit_solution(1183035205590962859)
XLA Ops:
  0.0 1.6 %copy.156 = bf16[16,2,8,256]{3,2,0,1:T(8,128)(2,1)} copy(bf16[16,2,8,256]{3,2,1,0:T(8,128)(2,1)} %bitcast.194) | data formatting | bytes 262144 | tf_op jit(solution)/shard_map/all_to_all | solution.py:94
  1.6 4.0 %all-to-all-start = ((bf16[128,2,256]{2,0,1:T(8,128)(2,1)}), bf16[128,2,256]{2,0,1:T(8,128)(2,1)S(1)}, u32[]{:S(2)}, u32[]{:S(2)}) async-start(bf16[128,2,256]{2,0,1:T(8,128)(2,1)} %bitcast.172), calls=%async_computation | async-start | bytes 262144 | tf_op jit(solution)/shard_map/all_to_all | solution.py:94
  5.6 1.7 %copy.117 = bf16[128,512]{0,1:T(8,128)(2,1)} copy(bf16[128,512]{1,0:T(8,128)(2,1)} %param.7) | data formatting | bytes 262144 | tf_op args[2]
  7.3 3.4 %all-to-all-start.2 = ((bf16[128,2,256]{0,2,1:T(8,128)(2,1)}), bf16[128,2,256]{0,2,1:T(8,128)(2,1)S(1)}, u32[]{:S(2)}, u32[]{:S(2)}) async-start(bf16[128,2,256]{0,2,1:T(8,128)(2,1)} %bitcast.7), calls=%async_computation.2 | async-start | bytes 262144 | tf_op jit(solution)/shard_map/all_to_all | solution.py:95
  10.9 0.3 multiply_reduce_fusion.1
  11.3 0.5 %multiply_cosine_fusion = (f32[256,64]{1,0:T(8,128)S(1)}, f32[256,64]{1,0:T(8,128)S(1)}) fusion(f32[64]{0:T(128)S(1)} %multiply_exponential_fusion, f32[256]{0:T(256)S(1)} %get-tuple-element.76), kind=kLoop, calls=%fused_computation.77 | loop fusion | flops 16384 | bytes 132352 | tf_op jit(solution)/shard_map/cos | solution.py:30
  12.7 0.7 %fusion.47 = bf16[2,128,256]{1,2,0:T(8,128)(2,1)} fusion(bf16[1,256,256]{1,2,0:T(8,128)(2,1)S(1)} %bitcast.184, bf16[1,256,256]{1,2,0:T(8,128)(2,1)S(1)} %copy.121), kind=kLoop, calls=%fused_computation.78 | loop fusion | flops 65536 | bytes 393216 | tf_op jit(solution)/shard_map/stack | solution.py:131
  13.3 3.1 %collective-permute-start = (bf16[2,128,256]{1,2,0:T(8,128)(2,1)}, bf16[2,128,256]{1,2,0:T(8,128)(2,1)}, u32[]{:S(2)}, u32[]{:S(2)}) collective-permute-start(bf16[2,128,256]{1,2,0:T(8,128)(2,1)} %fusion.47), channel_id=1, source_target_pairs={{0,2},{2,4},{4,6},{6,8},{8,10},{10,12},{12,14},{1,3},{3,5},{5,7},{... | collective-permute-start | bytes 393224 | tf_op jit(solution)/shard_map/while/body/eval_jaxpr/ppermute | solution.py:15
  16.4 2.3 %copy.155 = bf16[16,2,8,2048]{3,2,0,1:T(8,128)(2,1)} copy(bf16[16,2,8,2048]{3,2,1,0:T(8,128)(2,1)} %bitcast.186) | data formatting | bytes 2097152 | tf_op jit(solution)/shard_map/all_to_all | solution.py:93
  18.8 3.9 %all-to-all-start.1 = ((bf16[128,2,2048]{2,0,1:T(8,128)(2,1)}), bf16[128,2,2048]{2,0,1:T(8,128)(2,1)S(1)}, u32[]{:S(2)}, u32[]{:S(2)}) async-start(bf16[128,2,2048]{2,0,1:T(8,128)(2,1)} %bitcast.171), calls=%async_computation.1 | async-start | bytes 2097152 | tf_op jit(solution)/shard_map/all_to_all | solution.py:93
  22.6 0.7 %pad_maximum_fusion.2 = bf16[2,256,256]{1,2,0:T(8,128)(2,1)} fusion(bf16[1,256,256]{1,2,0:T(8,128)(2,1)S(1)} %copy.121, bf16[1,256,256]{1,2,0:T(8,128)(2,1)S(1)} %bitcast.185), kind=kLoop, calls=%fused_computation.54 | loop fusion | flops 131072 | bytes 524288 | tf_op jit(solution)/shard_map/stack | solution.py:131
  23.4 3.1 %collective-permute-start.1 = (bf16[2,256,256]{1,2,0:T(8,128)(2,1)}, bf16[2,256,256]{1,2,0:T(8,128)(2,1)}, u32[]{:S(2)}, u32[]{:S(2)}) collective-permute-start(bf16[2,256,256]{1,2,0:T(8,128)(2,1)} %pad_maximum_fusion.2), channel_id=1, source_target_pairs={{2,0},{4,2},{6,4},{8,6},{10,8},{12,10},{14,12},{3,1},{5,3},{7,5},{... | collective-permute-start | bytes 786440 | tf_op jit(solution)/shard_map/while/body/eval_jaxpr/ppermute | solution.py:15
  26.8 0.4 copy.149
  27.2 0.6 %multiply_reduce_fusion = f32[256,16]{1,0:T(8,128)S(1)} fusion(f32[256,16,128]{2,1,0:T(8,128)S(1)} %bitcast.173), kind=kLoop, calls=%fused_computation.10 | loop fusion | flops 1044480 | bytes 2113536 | tf_op jit(solution)/shard_map/reduce_sum | solution.py:23
  28.1 0.9 %multiply_multiply_fusion = f32[256,16,128]{2,1,0:T(8,128)S(1)} fusion(f32[128]{0:T(128)S(1)} %copy-done.7, f32[256,16]{1,0:T(8,128)S(1)} %copy.115, f32[32,8,16,128]{3,2,1,0:T(8,128)S(1)} %copy.149), kind=kLoop, calls=%fused_computation.9 | loop fusion | flops 1048576 | bytes 4211200 | tf_op jit(solution)/shard_map/mul | solution.py:24
  28.9 0.8 %subtract_convert_fusion = (bf16[256,16,64]{2,1,0:T(8,128)(2,1)S(1)}, bf16[256,16,64]{2,1,0:T(8,128)(2,1)S(1)}) fusion(f32[256,16,128]{2,1,0:T(8,128)S(1)} %multiply_multiply_fusion, f32[256,64]{1,0:T(8,128)S(1)} %get-tuple-element.74, f32[256,64]{1,0:T(8,128)S(1)} %get-tuple-element.73), kind=kLoop, calls=%fused_computation.8 | loop fusion | flops 2097152 | bytes 3276800 | tf_op jit(solution)/shard_map/convert.4
  29.7 0.6 %fusion.36 = (bf16[128,16,128]{2,1,0:T(8,128)(2,1)S(1)}, bf16[128,16,128]{2,1,0:T(8,128)(2,1)S(1)}) fusion(bf16[256,16,64]{2,1,0:T(8,128)(2,1)S(1)} %get-tuple-element.39, bf16[256,16,64]{2,1,0:T(8,128)(2,1)S(1)} %get-tuple-element.40), kind=kLoop, calls=%fused_computation.49 | loop fusion | flops 2097152 | bytes 2097152 | tf_op jit(solution)/shard_map/concatenate | solution.py:34
  30.5 0.9 %copy.124 = bf16[128,16,128]{2,0,1:T(8,128)(2,1)} copy(bf16[128,16,128]{2,1,0:T(8,128)(2,1)S(1)} %get-tuple-element.42) | data formatting | bytes 1048576 | tf_op jit(solution)/shard_map/slice | solution.py:100
  31.5 0.7 %reshape.252 = bf16[256,2,128,1]{0,2,1,3:T(8,128)(2,1)} reshape(bf16[2,128,256]{1,0,2:T(2,128)(2,1)S(1)} %copy.125) | data formatting | bytes 262144 | tf_op jit(solution)/shard_map/reshape | solution.py:50
  32.7 1.5 %fusion.73 = (f32[2,8,128]{2,1,0:T(8,128)S(1)}, f32[2,8,128,256]{2,3,1,0:T(8,128)S(1)}) fusion(bf16[128,2,8,128]{3,0,2,1:T(8,128)(2,1)} %bitcast.177, bf16[256,2,128]{2,0,1:T(8,128)(2,1)S(1)} %maximum_convert_fusion, pred[128,256]{0,1:T(8,128)(4,1)S(1)} %fusion.50), kind=kOutput, calls=%fused_computation.128 | convolution fusion | flops 135788544 | bytes 2793472 | tf_op jit(solution)/shard_map/rkgd,nkd->kgrn/dot_general | solution.py:51
  34.4 1.5 %fusion.72 = (bf16[1,128,256]{1,2,0:T(8,128)(2,1)}, bf16[1,128,256]{1,2,0:T(8,128)(2,1)S(1)}) fusion(bf16[2,128,256]{1,2,0:T(8,128)(2,1)} %collective-permute-done), kind=kLoop, calls=%fused_computation.127 | loop fusion | bytes 262144 | tf_op jit(solution)/shard_map/while/body/eval_jaxpr/slice | solution.py:150
  36.1 1.4 %fusion.75 = (f32[2,8,128]{2,1,0:T(8,128)S(1)}, f32[2,8,128,128]{2,3,1,0:T(8,128)S(1)}) fusion(bf16[128,2,128,1]{0,2,3,1:T(8,128)(2,1)S(1)} %bitcast.188, bf16[128,2,8,128]{3,0,2,1:T(8,128)(2,1)} %bitcast.176, pred[128,128]{0,1:T(8,128)(4,1)S(1)} %get-tuple-element.77), kind=kOutput, calls=%fused_computation.130 | convolution fusion | flops 67893248 | bytes 1662976 | tf_op jit(solution)/shard_map/while/body/eval_jaxpr/rkgd,nkd->kgrn/dot_general | solution.py:51
  37.8 0.3 fusion.16
  38.7 1.6 %fusion.71 = (bf16[1,256,256]{1,2,0:T(8,128)(2,1)}, bf16[1,256,256]{1,2,0:T(8,128)(2,1)S(1)}) fusion(bf16[2,256,256]{1,2,0:T(8,128)(2,1)} %collective-permute-done.1), kind=kLoop, calls=%fused_computation.126 | loop fusion | bytes 524288 | tf_op jit(solution)/shard_map/while/body/eval_jaxpr/slice | solution.py:155
  40.4 0.6 %fusion.2 = (f32[2,8,128]{2,1,0:T(8,128)S(1)}, f32[2,384,128,8]{2,1,3,0:T(8,128)S(1)}) fusion(pred[128,384]{0,1:T(8,128)(4,1)S(1)} %fusion.46, bf16[128,2,8,128]{3,0,2,1:T(8,128)(2,1)S(1)} %bitcast.178, bf16[256,2,128]{2,0,1:T(8,128)(2,1)S(1)} %copy.128, bf16[128,2,128]{2,0,1:T(8,128)(2,1)S(1)} %copy.127), kind=kOutput, calls=%fused_computation.4 | convolution fusion | flops 204077056 | bytes 3923968 | tf_op jit(solution)/shard_map/while/body/eval_jaxpr/rkgd,nkd->kgrn/dot_general | solution.py:51
  41.4 0.7 %fusion = f32[2,8,128]{2,1,0:T(8,128)S(1)} fusion(f32[2,384,128,8]{2,1,3,0:T(8,128)S(1)} %get-tuple-element.82, f32[2,8,128]{2,1,0:T(8,128)S(1)} %get-tuple-element.72, pred[128,384]{0,1:T(8,128)(4,1)S(1)} %fusion.46), kind=kLoop, calls=%fused_computation.2 | loop fusion | flops 3143680 | bytes 3211264 | tf_op jit(solution)/shard_map/while/body/eval_jaxpr/reduce_sum | solution.py:60
  42.3 0.9 %fusion.19 = f32[128,2,8,128]{0,3,2,1:T(8,128)S(1)} fusion(f32[2,384,128,8]{2,1,3,0:T(8,128)S(1)} %get-tuple-element.82, f32[2,8,128]{2,1,0:T(8,128)S(1)} %get-tuple-element.72, pred[128,384]{0,1:T(8,128)(4,1)S(1)} %fusion.46, bf16[256,2,128]{0,2,1:T(8,128)(2,1)S(1)} %bitcast.195, bf16[128,2,128]{0,2,1:T(8,128)(2,1)S(1)} %bitcast.197), kind=kOutput, calls=%fused_computation.29 | convolution fusion | flops 204865536 | bytes 4448256 | tf_op jit(solution)/shard_map/while/body/eval_jaxpr/kgrn,nkd->kgrd/dot_general | solution.py:61
  43.2 0.5 %fusion.27 = bf16[128,2,8,128]{0,3,2,1:T(8,128)(2,1)S(1)} fusion(f32[128,2,8,128]{0,3,2,1:T(8,128)S(1)} %fusion.19, f32[2,8,128,256]{2,3,1,0:T(8,128)S(1)} %get-tuple-element.80, f32[2,8,128]{2,1,0:T(8,128)S(1)} %get-tuple-element.71, f32[128,2,8]{0,2,1:T(8,128)S(1)} %get-tuple-element.37, f32[128,2,8]{0,2,1:T(8,128)S(1)} %get-tuple-element.38, ...), kind=kOutput, calls=%fused_computation.37 | convolution fusion | flops 136577024 | bytes 3833856 | tf_op jit(solution)/shard_map/kgrn,nkd->kgrd/dot_general | solution.py:61
  43.9 0.6 %copy.130 = bf16[256,2048]{1,0:T(8,128)(2,1)S(1)} copy(bf16[256,2048]{0,1:T(8,128)(2,1)S(1)} %pad_maximum_fusion) | data formatting | bytes 2097152 | tf_op jit(solution)/shard_map/concatenate | solution.py:173
  44.5 4.5 %all_to_all.61 = bf16[2,128,2048]{2,1,0:T(8,128)(2,1)S(1)} all-to-all(bf16[2,128,2048]{2,1,0:T(8,128)(2,1)S(1)} %bitcast.179), channel_id=1, replica_groups=mesh['groups'=2,'blk'=8,'uly'=2] {'uly'}, dimensions={0} | all-to-all | bytes 2097152 | tf_op jit(solution)/shard_map/all_to_all | solution.py:174
  49.0 0.7 %copy.131 = bf16[2,128,2048]{1,2,0:T(8,128)(2,1)S(1)} copy(bf16[2,128,2048]{2,1,0:T(8,128)(2,1)S(1)} %all_to_all.61) | data formatting | bytes 2097152 | tf_op jit(solution)/shard_map/all_to_all | solution.py:174
  49.7 1.3 %copy.132 = bf16[128,4096]{1,0:T(8,128)(2,1)} copy(bf16[128,4096]{0,1:T(8,128)(2,1)S(1)} %bitcast.180) | data formatting | bytes 2097152 | tf_op jit(solution)/shard_map/all_to_all | solution.py:174
  (61 shorter events, 4.1 us)
Async XLA Ops:
  0.0 11.9 %copy-start.6 = (f32[128]{0:T(128)S(1)}, f32[128]{0:T(128)}, u32[]{:S(2)}) copy-start(f32[128]{0:T(128)} %param.9) | copy-start | bytes 1540
  1.6 5.7 %all-to-all-start = ((bf16[128,2,256]{2,0,1:T(8,128)(2,1)}), bf16[128,2,256]{2,0,1:T(8,128)(2,1)S(1)}, u32[]{:S(2)}, u32[]{:S(2)}) async-start(bf16[128,2,256]{2,0,1:T(8,128)(2,1)} %bitcast.172), calls=%async_computation | async-start | bytes 262144 | tf_op jit(solution)/shard_map/all_to_all | solution.py:94
  7.3 5.1 %all-to-all-start.2 = ((bf16[128,2,256]{0,2,1:T(8,128)(2,1)}), bf16[128,2,256]{0,2,1:T(8,128)(2,1)S(1)}, u32[]{:S(2)}, u32[]{:S(2)}) async-start(bf16[128,2,256]{0,2,1:T(8,128)(2,1)} %bitcast.7), calls=%async_computation.2 | async-start | bytes 262144 | tf_op jit(solution)/shard_map/all_to_all | solution.py:95
  13.3 21.1 %collective-permute-start = (bf16[2,128,256]{1,2,0:T(8,128)(2,1)}, bf16[2,128,256]{1,2,0:T(8,128)(2,1)}, u32[]{:S(2)}, u32[]{:S(2)}) collective-permute-start(bf16[2,128,256]{1,2,0:T(8,128)(2,1)} %fusion.47), channel_id=1, source_target_pairs={{0,2},{2,4},{4,6},{6,8},{8,10},{10,12},{12,14},{1,3},{3,5},{5,7},{... | collective-permute-start | bytes 393224 | tf_op jit(solution)/shard_map/while/body/eval_jaxpr/ppermute | solution.py:15
  18.8 7.8 %all-to-all-start.1 = ((bf16[128,2,2048]{2,0,1:T(8,128)(2,1)}), bf16[128,2,2048]{2,0,1:T(8,128)(2,1)S(1)}, u32[]{:S(2)}, u32[]{:S(2)}) async-start(bf16[128,2,2048]{2,0,1:T(8,128)(2,1)} %bitcast.171), calls=%async_computation.1 | async-start | bytes 2097152 | tf_op jit(solution)/shard_map/all_to_all | solution.py:93
  23.4 15.3 %collective-permute-start.1 = (bf16[2,256,256]{1,2,0:T(8,128)(2,1)}, bf16[2,256,256]{1,2,0:T(8,128)(2,1)}, u32[]{:S(2)}, u32[]{:S(2)}) collective-permute-start(bf16[2,256,256]{1,2,0:T(8,128)(2,1)} %pad_maximum_fusion.2), channel_id=1, source_target_pairs={{2,0},{4,2},{6,4},{8,6},{10,8},{12,10},{14,12},{3,1},{5,3},{7,5},{... | collective-permute-start | bytes 786440 | tf_op jit(solution)/shard_map/while/body/eval_jaxpr/ppermute | solution.py:15
  27.2 0.8 %copy-start.7 = (f32[128]{0:T(128)S(1)}, f32[128]{0:T(128)}, u32[]{:S(2)}) copy-start(f32[128]{0:T(128)} %param.8) | copy-start | bytes 1540
  30.4 2.2 %copy-start = (bf16[128,16,128]{2,0,1:T(8,128)(2,1)}, bf16[128,16,128]{2,0,1:T(8,128)(2,1)S(1)}, u32[]{:S(2)}) copy-start(bf16[128,16,128]{2,0,1:T(8,128)(2,1)S(1)} %copy.116) | copy-start | bytes 1572868
  37.5 0.8 %copy-start.4 = (bf16[1,128,256]{1,2,0:T(8,128)(2,1)S(1)}, bf16[1,128,256]{1,2,0:T(8,128)(2,1)}, u32[]{:S(2)}) copy-start(bf16[1,128,256]{1,2,0:T(8,128)(2,1)} %get-tuple-element.47) | copy-start | bytes 196612
  38.3 2.1 %copy-start.1 = (bf16[128,16,128]{2,0,1:T(8,128)(2,1)S(1)}, bf16[128,16,128]{2,0,1:T(8,128)(2,1)}, u32[]{:S(2)}) copy-start(bf16[128,16,128]{2,0,1:T(8,128)(2,1)} %copy.124) | copy-start | bytes 1572868
  41.4 0.9 %copy-start.3 = (bf16[1,256,256]{1,2,0:T(8,128)(2,1)S(1)}, bf16[1,256,256]{1,2,0:T(8,128)(2,1)}, u32[]{:S(2)}) copy-start(bf16[1,256,256]{1,2,0:T(8,128)(2,1)} %get-tuple-element.45) | copy-start | bytes 393220
  41.4 0.9 %copy-start.5 = (bf16[1,128,256]{1,2,0:T(8,128)(2,1)S(1)}, bf16[1,128,256]{1,2,0:T(8,128)(2,1)}, u32[]{:S(2)}) copy-start(bf16[1,128,256]{1,2,0:T(8,128)(2,1)} %get-tuple-element.47) | copy-start | bytes 196612
  42.3 0.9 %copy-start.2 = (bf16[256,2,128,1]{0,2,1,3:T(8,128)(2,1)S(1)}, bf16[256,2,128,1]{0,2,1,3:T(8,128)(2,1)}, u32[]{:S(2)}) copy-start(bf16[256,2,128,1]{0,2,1,3:T(8,128)(2,1)} %reshape.252) | copy-start | bytes 393220
where the time goes:
time: 51.7 us; the launch traced here: 51 us
  starting transfers between devices  17.5 us (34%)
  local copies, waits for them, and re-layouts  15 us (29%)
  other arithmetic  7.62 us (15%)
  matrix products  5.9 us (11%)
  blocking collectives  4.51 us (9%)
  between operations  0.52 us (1%)
    ppermute x2, starting transfers between devices, shifted(): return lax.ppermute(block, axis, route)  6.16 us
    all_to_all x1, blocking collectives, local(): lax.all_to_all(merged, 'uly', split_axis=0, concat_axis=1, tiled=True)  4.51 us
    all_to_all x1, starting transfers between devices, local(): lax.all_to_all(key_proj, 'uly', split_axis=1, concat_axis=0, tiled=True)  4.04 us
    all_to_all x1, starting transfers between devices, local(): lax.all_to_all(query_proj, 'uly', split_axis=1, concat_axis=0, tiled=True)  3.87 us
    dot_general x4, matrix products, attend(): jnp.einsum('rkgd,nkd->kgrn', query_heads, key_heads, preferred_element_ty...  3.8 us
    all_to_all x1, starting transfers between devices, local(): lax.all_to_all(value_projection, 'uly', split_axis=1, concat_axis=0, tile...  3.4 us
    unnamed x18, local copies, waits for them, and re-layouts  2.42 us
    all_to_all x1, local copies, waits for them, and re-layouts, local(): lax.all_to_all(query_proj, 'uly', split_axis=1, concat_axis=0, tiled=True)  2.31 us
  transfers between devices with their start and end apart: 5, of which 0 were waited for; matrix products, arithmetic and copies ran while one was open for 36% of the time, Pallas kernels for 0%

commit v1 on v0

v1 whole, which is shorter than its diff:
```python
import functools
import math

import jax
import jax.numpy as jnp
from jax import lax
from jax.experimental import pallas as pl
from jax.experimental.pallas import tpu as pltpu
from jax.sharding import PartitionSpec as P

NEG_FILL = -1e30
ROPE_BASE = 1000000.0
EPS = 1e-06
MESH = pl.DeviceIdType.MESH


def rope_tables(first_pos, rows, frequency, sign, gain, gain_swapped):
    eight = lax.broadcasted_iota(jnp.int32, (8, 128), 0).astype(jnp.float32)
    fine = eight * frequency
    fine_cos, fine_sin = jnp.cos(fine), jnp.sin(fine)
    steps = rows // 8
    coarse_pos = first_pos + 8 * lax.broadcasted_iota(jnp.int32, (steps, 128), 0)
    coarse = coarse_pos.astype(jnp.float32) * frequency
    coarse_cos, coarse_sin = jnp.cos(coarse), jnp.sin(coarse)
    cosines, sines = [], []
    for j in range(steps):
        cos_j, sin_j = coarse_cos[j : j + 1], coarse_sin[j : j + 1]
        cosines.append((cos_j * fine_cos - sin_j * fine_sin) * gain)
        sines.append((sin_j * fine_cos + cos_j * fine_sin) * (sign * gain_swapped))
    return jnp.concatenate(cosines), jnp.concatenate(sines)


def rotate(x, table_a, table_b):
    x = x.astype(jnp.float32)
    r = lax.rsqrt(jnp.mean(x * x, axis=-1, keepdims=True) + EPS)
    swapped = pltpu.roll(x, x.shape[1] // 2, 1)
    return ((x * table_a + swapped * table_b) * r).astype(jnp.bfloat16)


def kernel(
    cycle, span, kv_heads, group,
    q_hbm, k_hbm, v_hbm, qg_hbm, kg_hbm, o_ref,
    q_buf, kv_own, kv_prev, q_rot, k_cat, v_cat, tab, gains,
    q_sem, own_sem, gain_sem, send_sem, recv_sem,
):
    rows, head = k_hbm.shape[0], qg_hbm.shape[1]
    width = group * head
    blk, uly = lax.axis_index("blk"), lax.axis_index("uly")
    last = 2 * cycle - 1
    stretch = jnp.where(uly == 0, blk, last - blk)

    def device_of(index):
        low = index < cycle
        return {"blk": jnp.where(low, index, last - index), "uly": jnp.where(low, 0, 1)}

    barrier = pltpu.get_barrier_semaphore()
    for d in range(1, span + 1):

        @pl.when(stretch >= d)
        def _(d=d):
            pl.semaphore_signal(
                barrier, inc=1, device_id=device_of(stretch - d), device_id_type=MESH
            )

    own_copies = [
        pltpu.make_async_copy(src, kv_own.at[i], own_sem.at[i])
        for i, src in enumerate((k_hbm, v_hbm))
    ]
    q_copies = [
        pltpu.make_async_copy(
            q_hbm.at[:, pl.ds(h * width, width)], q_buf.at[h], q_sem.at[h]
        )
        for h in range(kv_heads)
    ]

    gain_copies = [
        pltpu.make_async_copy(src, gains.at[i], gain_sem.at[i])
        for i, src in enumerate((qg_hbm, kg_hbm))
    ]

    def remote(d, h, i):
        src = (k_hbm, v_hbm)[i]
        return pltpu.make_async_remote_copy(
            src_ref=src.at[:, pl.ds(h * head, head)],
            dst_ref=kv_prev.at[d - 1, i, h],
            send_sem=send_sem.at[d - 1, i, h],
            recv_sem=recv_sem.at[d - 1, i, h],
            device_id=device_of(stretch + d),
            device_id_type=MESH,
        )

    for copy in gain_copies + own_copies[:1] + q_copies + own_copies[1:]:
        copy.start()

    for d in range(1, span + 1):

        @pl.when(stretch + d <= last)
        def _():
            pl.semaphore_wait(barrier, 1)

    for h in range(kv_heads):
        for i in range(2):
            for d in range(1, span + 1):

                @pl.when(stretch + d <= last)
                def _(d=d, h=h, i=i):
                    remote(d, h, i).start()

    for d in range(1, span + 1):

        @pl.when(stretch < d)
        def _(d=d):
            kv_prev[d - 1] = jnp.zeros_like(kv_prev[d - 1])

    half = head // 2
    lane = lax.broadcasted_iota(jnp.int32, (1, head), 1)
    frequency = jnp.exp(
        lax.rem(lane, half).astype(jnp.float32) * (-2.0 * math.log(ROPE_BASE) / head)
    )
    sign = jnp.where(lane < half, -1.0, 1.0)
    for copy in gain_copies:
        copy.wait()
    q_gain, k_gain = gains[0], gains[1]
    q_swap, k_swap = pltpu.roll(q_gain, half, 1), pltpu.roll(k_gain, half, 1)
    tables = functools.partial(rope_tables, rows=rows, frequency=frequency, sign=sign)
    tab[0, 0], tab[0, 1] = tables(stretch * rows, gain=q_gain, gain_swapped=q_swap)
    for d in range(span + 1):
        tab[d + 1, 0], tab[d + 1, 1] = tables(
            (stretch - d) * rows, gain=k_gain, gain_swapped=k_swap
        )

    own_copies[0].wait()
    for h in range(kv_heads):
        k_cat[h, :rows] = rotate(
            kv_own[0, :, h * head : (h + 1) * head], tab[1, 0], tab[1, 1]
        )
    for h in range(kv_heads):
        q_copies[h].wait()
        for g in range(group):
            q_rot[h, g * rows : (g + 1) * rows] = rotate(
                q_buf[h, :, g * head : (g + 1) * head], tab[0, 0], tab[0, 1]
            )
    own_copies[1].wait()
    for h in range(kv_heads):
        v_cat[h, :rows] = kv_own[1, :, h * head : (h + 1) * head]

    row = lax.broadcasted_iota(jnp.int32, (rows, rows), 0)
    col = lax.broadcasted_iota(jnp.int32, (rows, rows), 1)
    own = col <= row
    scale = 1.0 / math.sqrt(head)
    bias = [
        jnp.where(stretch >= d, 0.0, NEG_FILL).astype(jnp.float32)
        for d in range(1, span + 1)
    ]

    for h in range(kv_heads):
        for d in range(1, span + 1):

            @pl.when(stretch >= d)
            def _(d=d, h=h):
                remote(d, h, 0).wait_recv()

            k_cat[h, d * rows : (d + 1) * rows] = rotate(
                kv_prev[d - 1, 0, h], tab[d + 1, 0], tab[d + 1, 1]
            )

            @pl.when(stretch >= d)
            def _(d=d, h=h):
                remote(d, h, 1).wait_recv()

            v_cat[h, d * rows : (d + 1) * rows] = kv_prev[d - 1, 1, h]

        keys, values = k_cat[h], v_cat[h]
        for g in range(group):
            scores = lax.dot_general(
                q_rot[h, g * rows : (g + 1) * rows],
                keys,
                (((1,), (1,)), ((), ())),
                preferred_element_type=jnp.float32,
            )
            parts = [scores[:, d * rows : (d + 1) * rows] for d in range(span + 1)]
            tiles = [jnp.where(own, parts[0], parts[span] + bias[span - 1])]
            tiles += [parts[d] + bias[d - 1] for d in range(1, span)]
            top = functools.reduce(jnp.maximum, tiles)
            top = jnp.max(top, axis=-1, keepdims=True)
            weights = [jnp.exp((tile - top) * scale) for tile in tiles]
            total = jnp.sum(functools.reduce(jnp.add, weights), axis=-1, keepdims=True)
            near = jnp.where(own, weights[0], 0.0)
            far = jnp.where(own, 0.0, weights[0])
            rounded = jnp.concatenate([near] + weights[1:] + [far], axis=1)
            mixed = jnp.dot(
                rounded.astype(jnp.bfloat16), values, preferred_element_type=jnp.float32
            )
            o_ref[:, h * width + g * head : h * width + (g + 1) * head] = (
                mixed / total
            ).astype(o_ref.dtype)

    for h in range(kv_heads):
        for i in range(2):
            for d in range(1, span + 1):

                @pl.when(stretch + d <= last)
                def _(d=d, h=h, i=i):
                    remote(d, h, i).wait_send()


def local(query_proj, key_proj, value_projection, query_gain, key_gain):
    cycle = lax.axis_size("blk")
    span = max(1, cycle // 64)
    rows, head = query_proj.shape[0], query_gain.shape[0]
    kv_heads = key_proj.shape[1] // head
    group = query_proj.shape[1] // head // kv_heads
    bf16 = jnp.bfloat16
    vmem = pl.BlockSpec(memory_space=pltpu.VMEM)
    hbm = pl.BlockSpec(memory_space=pltpu.HBM)
    return pl.pallas_call(
        functools.partial(kernel, cycle, span, kv_heads, group),
        out_shape=jax.ShapeDtypeStruct(query_proj.shape, bf16),
        in_specs=[hbm] * 5,
        out_specs=vmem,
        scratch_shapes=[
            pltpu.VMEM((kv_heads, rows, group * head), bf16),
            pltpu.VMEM((2, rows, kv_heads * head), bf16),
            pltpu.VMEM((span, 2, kv_heads, rows, head), bf16),
            pltpu.VMEM((kv_heads, group * rows, head), bf16),
            pltpu.VMEM((kv_heads, (span + 1) * rows, head), bf16),
            pltpu.VMEM((kv_heads, (span + 1) * rows, head), bf16),
            pltpu.VMEM((span + 2, 2, rows, head), jnp.float32),
            pltpu.VMEM((2, 1, head), jnp.float32),
            pltpu.SemaphoreType.DMA((kv_heads,)),
            pltpu.SemaphoreType.DMA((2,)),
            pltpu.SemaphoreType.DMA((2,)),
            pltpu.SemaphoreType.DMA((span, 2, kv_heads)),
            pltpu.SemaphoreType.DMA((span, 2, kv_heads)),
        ],
        compiler_params=pltpu.CompilerParams(
            collective_id=0, has_side_effects=True, vmem_limit_bytes=16 * 1024 * 1024
        ),
        name="window_attention",
    )(
        query_proj,
        key_proj,
        value_projection,
        query_gain.reshape(1, head),
        key_gain.reshape(1, head),
    )


def solution(mesh):
    rows = P(("groups", "blk", "uly"), None)
    return jax.shard_map(
        local,
        mesh=mesh,
        in_specs=(rows, rows, rows, P(), P()),
        out_specs=rows,
        check_vma=False,
    )
```

time: 51.7 us -> 15 us (0.29)
  the two profiles are of different devices: /device:TPU:25 before, /device:TPU:2 now
where the time goes in v1:
time: 15 us; the launch traced here: 14.8 us
  Pallas kernels  10.1 us (67%)
  local copies, waits for them, and re-layouts  4.67 us (31%)
    pallas_call x1, Pallas kernels, local(): pl.pallas_call(functools.partial(kernel, cycle, span, kv_heads, group), o...  10.1 us
    unnamed x11, local copies, waits for them, and re-layouts  4.67 us

profile of v1, /device:TPU:2, one launch (start us, length us, event | category | flops | bytes accessed | tf_op | source)
XLA Modules:
  0.0 14.8 jit_solution(11430689539050496963)
XLA Ops:
  0.0 0.0 copy-start.3
  0.0 0.0 copy-start.4
  0.0 0.7 %copy-done.3 = f32[128]{0:T(128)S(1)} copy-done((f32[128]{0:T(128)S(1)}, f32[128]{0:T(128)}, u32[]{:S(2)}) %copy-start.3) | copy-done | bytes 536
  0.7 0.0 copy-done.4
  0.7 0.0 copy-start
  0.7 1.2 %copy-done = bf16[128,4096]{1,0:T(8,128)(2,1)S(1)} copy-done((bf16[128,4096]{1,0:T(8,128)(2,1)S(1)}, bf16[128,4096]{1,0:T(8,128)(2,1)}, u32[]{:S(2)}) %copy-start) | copy-done | bytes 1048600
  1.9 0.0 copy-start.1
  1.9 0.9 %copy-done.1 = bf16[128,512]{1,0:T(8,128)(2,1)S(1)} copy-done((bf16[128,512]{1,0:T(8,128)(2,1)S(1)}, bf16[128,512]{1,0:T(8,128)(2,1)}, u32[]{:S(2)}) %copy-start.1) | copy-done | bytes 131096
  2.8 0.0 copy-start.2
  2.8 0.9 %copy-done.2 = bf16[128,512]{1,0:T(8,128)(2,1)S(1)} copy-done((bf16[128,512]{1,0:T(8,128)(2,1)S(1)}, bf16[128,512]{1,0:T(8,128)(2,1)}, u32[]{:S(2)}) %copy-start.2) | copy-done | bytes 131096
  3.7 10.1 %window_attention.1 = bf16[128,4096]{1,0:T(8,128)(2,1)S(1)} custom-call(bf16[128,4096]{1,0:T(8,128)(2,1)S(1)} %copy-done, bf16[128,512]{1,0:T(8,128)(2,1)S(1)} %copy-done.1, bf16[128,512]{1,0:T(8,128)(2,1)S(1)} %copy-done.2, f32[1,128]{1,0:T(1,128)S(1)} %bitcast.2, f32[1,128]{1,0:T(1,128)S(1)} %bitcast.3), custom_call_target="tpu_custom_call" | custom-call | tf_op jit(solution)/shard_map/window_attention/pallas_call | solution.py:216
  13.9 1.0 %copy.7 = bf16[128,4096]{1,0:T(8,128)(2,1)} copy(bf16[128,4096]{1,0:T(8,128)(2,1)S(1)} %window_attention.1) | data formatting | bytes 2097152
Async XLA Ops:
  0.0 0.7 %copy-start.3 = (f32[128]{0:T(128)S(1)}, f32[128]{0:T(128)}, u32[]{:S(2)}) copy-start(f32[128]{0:T(128)} %param.8) | copy-start | bytes 1540
  0.0 0.7 %copy-start.4 = (f32[128]{0:T(128)S(1)}, f32[128]{0:T(128)}, u32[]{:S(2)}) copy-start(f32[128]{0:T(128)} %param.9) | copy-start | bytes 1540
  0.7 1.2 %copy-start = (bf16[128,4096]{1,0:T(8,128)(2,1)S(1)}, bf16[128,4096]{1,0:T(8,128)(2,1)}, u32[]{:S(2)}) copy-start(bf16[128,4096]{1,0:T(8,128)(2,1)} %q_hbm.1) | copy-start | bytes 3145732
  1.9 0.9 %copy-start.1 = (bf16[128,512]{1,0:T(8,128)(2,1)S(1)}, bf16[128,512]{1,0:T(8,128)(2,1)}, u32[]{:S(2)}) copy-start(bf16[128,512]{1,0:T(8,128)(2,1)} %k_hbm.1) | copy-start | bytes 393220
  2.8 0.9 %copy-start.2 = (bf16[128,512]{1,0:T(8,128)(2,1)S(1)}, bf16[128,512]{1,0:T(8,128)(2,1)}, u32[]{:S(2)}) copy-start(bf16[128,512]{1,0:T(8,128)(2,1)} %v_hbm.1) | copy-start | bytes 393220

commit v2 on v1

--- a/solution.py
+++ b/solution.py
@@ -202,6 +202,10 @@
                 @pl.when(stretch + d <= last)
                 def _(d=d, h=h, i=i):
                     remote(d, h, i).wait_send()
+
+
+def in_hbm(array):
+    return pltpu.with_memory_space_constraint(array, pltpu.HBM)
 
 
 def local(query_proj, key_proj, value_projection, query_gain, key_gain):
@@ -238,11 +242,11 @@
         ),
         name="window_attention",
     )(
-        query_proj,
-        key_proj,
-        value_projection,
-        query_gain.reshape(1, head),
-        key_gain.reshape(1, head),
+        in_hbm(query_proj),
+        in_hbm(key_proj),
+        in_hbm(value_projection),
+        in_hbm(query_gain.reshape(1, head)),
+        in_hbm(key_gain.reshape(1, head)),
     )
 
 

time: 15 us -> 11.5 us (0.77)
  local copies, waits for them, and re-layouts: 4.67 us -> 0.97 us
  Pallas kernels: 10.1 us -> 10.4 us
    unnamed x11 -> x1, local copies, waits for them, and re-layouts: 4.67 us -> 0.97 us
    pallas_call x1, Pallas kernels: 10.1 us -> 10.4 us  [local(): pl.pallas_call(functools.partial(kernel, cycle, span, kv_heads, group), o...]
where the time goes in v2:
time: 11.5 us; the launch traced here: 11.3 us
  Pallas kernels  10.4 us (90%)
  local copies, waits for them, and re-layouts  0.97 us (8%)
    pallas_call x1, Pallas kernels, local(): pl.pallas_call(functools.partial(kernel, cycle, span, kv_heads, group), o...  10.4 us
    unnamed x1, local copies, waits for them, and re-layouts  0.97 us

profile of v2, /device:TPU:2, one launch (start us, length us, event | category | flops | bytes accessed | tf_op | source)
XLA Modules:
  0.0 11.3 jit_solution(657850979962624564)
XLA Ops:
  0.0 10.4 %window_attention.1 = bf16[128,4096]{1,0:T(8,128)(2,1)S(1)} custom-call(bf16[128,4096]{1,0:T(8,128)(2,1)} %q_hbm.1, bf16[128,512]{1,0:T(8,128)(2,1)} %k_hbm.1, bf16[128,512]{1,0:T(8,128)(2,1)} %v_hbm.1, f32[1,128]{1,0:T(1,128)} %bitcast.2, f32[1,128]{1,0:T(1,128)} %bitcast.3), custom_call_target="tpu_custom_call" | custom-call | tf_op jit(solution)/shard_map/window_attention/pallas_call | solution.py:220
  10.4 1.0 %copy.7 = bf16[128,4096]{1,0:T(8,128)(2,1)} copy(bf16[128,4096]{1,0:T(8,128)(2,1)S(1)} %window_attention.1) | data formatting | bytes 2097152
